TPU v7x, 256 devices: a whole 4x4x8 slice. The times are simulated.
256 devices in a mesh: area: 32 (over z, y_lo, core), win: 8 (over y_hi, x).
Axes of the slice: x: 4, y: 4 (y_hi: 2, y_lo: 2; y = y_hi * 2 + y_lo), z: 8, core: 2. Of those that a mesh axis runs over, the one named last changes fastest.
Arguments:
- kkt: bfloat16 [32, 8, 1536, 1536], P('area', 'win'), as said below
- offsets: float32 [32, 8, 1536, 256], P('area', 'win'), may hold values from -6 to 6
- lower: float32 [32, 8, 1536], P('area', 'win'), may hold values from -1.2 to -0.4
- upper: float32 [32, 8, 1536], P('area', 'win'), may hold values from 0.4 to 1.2
- partners: int32 [4, 32], replicated, may hold values from 0 to 31, as said below
- adjacency: int32 [32, 32], replicated, may hold values from 0 to 1, as said below
Outputs:
- consensus: float32 [32, 8, 1536, 256], P('area', 'win')
- duals: float32 [32, 8, 1536, 256], P('area', 'win')
Inputs may be any that keep to these rules, and one draw needn't show every extreme that they name: `partners`: row k is the perfect matching a -> a XOR c_k for a colour c_k between 1 and 31. `adjacency`: symmetric with a zero diagonal. `kkt`: each block is a dense full-rank matrix with a positive diagonal.
All inputs are finite; a program needn't handle non-finite values.
Results may differ from a plain program's by a relative error of at most 0.0028.
Values sent between devices are 32-bit elements; how exact they have to be, the bound alone decides.
No kernel may reach another device: no remote copies, remote signals or barrier semaphores. Data moves between devices by JAX's collectives and lax.ppermute only.
A program may use at most 64 MiB of HBM per device.

v0:
```python
import jax
import jax.numpy as jnp
from jax import lax
from jax.sharding import PartitionSpec as P

COUPLE = 512
BOUND = 256
ITERS = 4


def from_behind(array, axis, by):
    length = lax.axis_size(axis)
    pairs = [(i, i + by) for i in range(length) if 0 <= i + by < length]
    return lax.ppermute(array, axis, pairs)


def local(kkt, offsets, lower, upper, partners, adjacency):
    matrix = kkt[0, 0]
    costs = offsets[0, 0]
    low = lower[0, 0][:, None]
    high = upper[0, 0][:, None]
    sent = COUPLE + BOUND
    area = lax.axis_index("area")
    count = lax.axis_size("area")
    z_now = jnp.zeros_like(costs)
    u_now = jnp.zeros_like(costs)
    for step in range(ITERS):
        v_now = (costs + z_now - u_now).astype(jnp.bfloat16)
        x_full = jnp.dot(matrix, v_now, preferred_element_type=jnp.float32)
        x_head = x_full[:sent]
        y_head = jnp.minimum(jnp.maximum(x_head + u_now[:sent], low[:sent]), high[:sent])
        row = partners[step]
        mate = row[area]
        couple = y_head[:COUPLE]
        spread = lax.all_to_all(couple, "area", split_axis=0, concat_axis=0, tiled=True)
        pieces = spread.reshape(count, COUPLE // count, couple.shape[1])
        pieces = jnp.take(pieces, row, axis=0)
        other = lax.all_to_all(
            pieces.reshape(COUPLE, couple.shape[1]), "area", split_axis=0, concat_axis=0, tiled=True
        )
        linked = (adjacency[area, mate] == 1).astype(couple.dtype)
        new_couple = couple + linked * 0.5 * (other - couple)
        ends = y_head[COUPLE:sent]
        before = from_behind(ends, "win", 1)
        x_tail = x_full[sent:]
        y_tail = jnp.minimum(jnp.maximum(x_tail + u_now[sent:], low[sent:]), high[sent:])
        starts = 0.5 * (y_tail[:BOUND] + before)
        z_now = jnp.concatenate([new_couple, ends, starts, y_tail[BOUND:]], axis=0)
        u_now = u_now + x_full - z_now
    return (z_now[None, None], u_now[None, None])


def solution(mesh):
    in_specs = (
        P("area", "win", None, None),
        P("area", "win", None, None),
        P("area", "win", None),
        P("area", "win", None),
        P(),
        P(),
    )
    out_specs = (P("area", "win", None, None), P("area", "win", None, None))
    return jax.shard_map(local, mesh=mesh, in_specs=in_specs, out_specs=out_specs, check_vma=False)
```

profile of v0, /device:TPU:24, one launch (start us, length us, event | category | flops | bytes accessed | tf_op | source)
XLA Modules:
  0.0 237.5 jit_solution(11552726582234276036)
XLA Ops:
  1.4 4.2 %fusion.6 = f32[1536,256]{1,0:T(8,128)S(1)} fusion(bf16[1,1,1536,1536]{3,2,1,0:T(8,128)(2,1)} %param.8, f32[1,1,1536,256]{3,2,1,0:T(8,128)} %param.9), kind=kOutput, calls=%fused_computation.10 | convolution fusion | flops 1208352768 | bytes 7864320 | tf_op jit(solution)/shard_map/dot_general | solution.py:29
  7.8 10.1 %all-to-all-start = ((f32[32,16,256]{2,1,0:T(8,128)}), f32[32,16,256]{2,1,0:T(8,128)S(1)}, u32[]{:S(2)}, u32[]{:S(2)}) async-start(f32[32,16,256]{2,1,0:T(8,128)} %bitcast.6), calls=%async_computation | async-start | bytes 1048576 | tf_op jit(solution)/shard_map/all_to_all | solution.py:35
  18.0 17.6 %all-to-all-done = f32[32,16,256]{2,1,0:T(8,128)S(1)} async-done(((f32[32,16,256]{2,1,0:T(8,128)}), f32[32,16,256]{2,1,0:T(8,128)S(1)}, u32[]{:S(2)}, u32[]{:S(2)}) %all-to-all-start) | async-done | bytes 524320 | tf_op jit(solution)/shard_map/all_to_all | solution.py:35
  37.1 4.4 %all-to-all-start.1 = ((f32[32,16,256]{2,1,0:T(8,128)}), f32[32,16,256]{2,1,0:T(8,128)}, u32[]{:S(2)}, u32[]{:S(2)}) async-start(f32[32,16,256]{2,1,0:T(8,128)} %broadcast_select_fusion.3), calls=%async_computation.1 | async-start | bytes 1048576 | tf_op jit(solution)/shard_map/all_to_all | solution.py:38
  41.5 3.4 %collective-permute-start = (f32[256,256]{1,0:T(8,128)S(1)}, f32[256,256]{1,0:T(8,128)}, u32[]{:S(2)}, u32[]{:S(2)}) collective-permute-start(f32[256,256]{1,0:T(8,128)S(1)} %slice.178), channel_id=1, source_target_pairs={{0,1},{1,2},{2,3},{3,4},{4,5},{5,6},{6,7},{8,9},{9,10},{10,11},{11... | collective-permute-start | bytes 786440 | tf_op jit(solution)/shard_map/ppermute | solution.py:14
  54.4 1.5 fusion.59
  56.6 2.1 collective-permute-done
  62.2 4.4 %fusion.14 = f32[1536,256]{1,0:T(8,128)S(1)} fusion(bf16[1,1,1536,1536]{3,2,1,0:T(8,128)(2,1)} %param.8, f32[1536,256]{1,0:T(8,128)S(1)} %fusion.24, f32[1,1,1536,256]{3,2,1,0:T(8,128)S(1)} %copy-done.6, f32[512,256]{1,0:T(8,128)S(1)} %slice.181, f32[256,256]{1,0:T(8,128)S(1)} %fusion.55, f32[256,256]{1,0:T(8,128)S(1)} %slice.178, f32[512,256]{1,0:T(8,128)S(1)} %fusion.51), kind=kOutput, calls=%fused_computation.14 | convolution fusion | flops 1210318848 | bytes 11010048 | tf_op jit(solution)/shard_map/dot_general | solution.py:29
  68.7 7.8 %all-to-all-start.2 = ((f32[32,16,256]{2,1,0:T(8,128)}), f32[32,16,256]{2,1,0:T(8,128)S(1)}, u32[]{:S(2)}, u32[]{:S(2)}) async-start(f32[32,16,256]{2,1,0:T(8,128)} %bitcast.12), calls=%async_computation.2 | async-start | bytes 1048576 | tf_op jit(solution)/shard_map/all_to_all | solution.py:35
  76.5 17.7 %all-to-all-done.2 = f32[32,16,256]{2,1,0:T(8,128)S(1)} async-done(((f32[32,16,256]{2,1,0:T(8,128)}), f32[32,16,256]{2,1,0:T(8,128)S(1)}, u32[]{:S(2)}, u32[]{:S(2)}) %all-to-all-start.2) | async-done | bytes 524320 | tf_op jit(solution)/shard_map/all_to_all | solution.py:35
  95.7 4.4 %all-to-all-start.3 = ((f32[32,16,256]{2,1,0:T(8,128)}), f32[32,16,256]{2,1,0:T(8,128)}, u32[]{:S(2)}, u32[]{:S(2)}) async-start(f32[32,16,256]{2,1,0:T(8,128)} %broadcast_select_fusion.2), calls=%async_computation.3 | async-start | bytes 1048576 | tf_op jit(solution)/shard_map/all_to_all | solution.py:38
  100.1 1.9 collective-permute-start.1
  102.8 14.0 %collective-permute-done.1 = f32[256,256]{1,0:T(8,128)S(1)} collective-permute-done((f32[256,256]{1,0:T(8,128)S(1)}, f32[256,256]{1,0:T(8,128)S(1)}, u32[]{:S(2)}, u32[]{:S(2)}) %collective-permute-start.1) | collective-permute-done | bytes 262176 | tf_op jit(solution)/shard_map/ppermute | solution.py:14
  119.2 2.3 add_subtract_fusion.1
  125.6 6.3 %all-to-all-start.4 = ((f32[32,16,256]{2,1,0:T(8,128)}), f32[32,16,256]{2,1,0:T(8,128)S(1)}, u32[]{:S(2)}, u32[]{:S(2)}) async-start(f32[32,16,256]{2,1,0:T(8,128)} %bitcast.18), calls=%async_computation.4 | async-start | bytes 1048576 | tf_op jit(solution)/shard_map/all_to_all | solution.py:35
  131.9 17.7 %all-to-all-done.4 = f32[32,16,256]{2,1,0:T(8,128)S(1)} async-done(((f32[32,16,256]{2,1,0:T(8,128)}), f32[32,16,256]{2,1,0:T(8,128)S(1)}, u32[]{:S(2)}, u32[]{:S(2)}) %all-to-all-start.4) | async-done | bytes 524320 | tf_op jit(solution)/shard_map/all_to_all | solution.py:35
  150.9 1.9 broadcast_select_fusion.1
  152.9 4.4 %all-to-all-start.5 = ((f32[32,16,256]{2,1,0:T(8,128)}), f32[32,16,256]{2,1,0:T(8,128)}, u32[]{:S(2)}, u32[]{:S(2)}) async-start(f32[32,16,256]{2,1,0:T(8,128)} %broadcast_select_fusion.1), calls=%async_computation.5 | async-start | bytes 1048576 | tf_op jit(solution)/shard_map/all_to_all | solution.py:38
  157.3 2.1 collective-permute-start.2
  161.1 12.1 %collective-permute-done.2 = f32[256,256]{1,0:T(8,128)S(1)} collective-permute-done((f32[256,256]{1,0:T(8,128)S(1)}, f32[256,256]{1,0:T(8,128)S(1)}, u32[]{:S(2)}, u32[]{:S(2)}) %collective-permute-start.2) | collective-permute-done | bytes 262176 | tf_op jit(solution)/shard_map/ppermute | solution.py:14
  173.2 1.7 fusion.53
  176.7 1.7 add_subtract_fusion
  178.9 2.8 %fusion.8 = f32[1536,256]{1,0:T(8,128)S(1)} fusion(bf16[1,1,1536,1536]{3,2,1,0:T(8,128)(2,1)S(1)} %bitcast.98, f32[1536,256]{1,0:T(8,128)S(1)} %add_subtract_fusion, f32[1,1,1536,256]{3,2,1,0:T(8,128)S(1)} %copy-done.8, f32[512,256]{1,0:T(8,128)} %copy-done.10, f32[256,256]{1,0:T(8,128)S(1)} %copy-done.11, f32[256,256]{1,0:T(8,128)S(1)} %copy-done.13, ...), kind=kOutput, calls=%fused_computation.12 | convolution fusion | flops 1210318848 | bytes 11010048 | tf_op jit(solution)/shard_map/dot_general | solution.py:29
  183.9 6.9 %all-to-all-start.6 = ((f32[32,16,256]{2,1,0:T(8,128)}), f32[32,16,256]{2,1,0:T(8,128)S(1)}, u32[]{:S(2)}, u32[]{:S(2)}) async-start(f32[32,16,256]{2,1,0:T(8,128)} %bitcast.99), calls=%async_computation.6 | async-start | bytes 1048576 | tf_op jit(solution)/shard_map/all_to_all | solution.py:35
  190.9 17.7 %all-to-all-done.6 = f32[32,16,256]{2,1,0:T(8,128)S(1)} async-done(((f32[32,16,256]{2,1,0:T(8,128)}), f32[32,16,256]{2,1,0:T(8,128)S(1)}, u32[]{:S(2)}, u32[]{:S(2)}) %all-to-all-start.6) | async-done | bytes 524320 | tf_op jit(solution)/shard_map/all_to_all | solution.py:35
  209.9 2.0 broadcast_select_fusion
  211.9 4.4 %all-to-all-start.7 = ((f32[32,16,256]{2,1,0:T(8,128)}), f32[32,16,256]{2,1,0:T(8,128)}, u32[]{:S(2)}, u32[]{:S(2)}) async-start(f32[32,16,256]{2,1,0:T(8,128)} %broadcast_select_fusion), calls=%async_computation.7 | async-start | bytes 1048576 | tf_op jit(solution)/shard_map/all_to_all | solution.py:38
  216.4 1.9 collective-permute-start.3
  218.9 2.0 slice.205
  220.9 9.9 %collective-permute-done.3 = f32[256,256]{1,0:T(8,128)S(1)} collective-permute-done((f32[256,256]{1,0:T(8,128)S(1)}, f32[256,256]{1,0:T(8,128)S(1)}, u32[]{:S(2)}, u32[]{:S(2)}) %collective-permute-start.3) | collective-permute-done | bytes 262176 | tf_op jit(solution)/shard_map/ppermute | solution.py:14
  231.9 2.3 all-to-all-done.7
  235.6 2.0 subtract_bitcast_fusion
  (88 shorter events, 31.2 us)
Async XLA Ops:
  7.0 10.9 %copy-start.17 = (s32[4,32]{1,0:T(4,128)S(1)}, s32[4,32]{1,0:T(4,128)}, u32[]{:S(2)}) copy-start(s32[4,32]{1,0:T(4,128)} %param.12) | copy-start | bytes 1540
  7.8 27.8 %all-to-all-start = ((f32[32,16,256]{2,1,0:T(8,128)}), f32[32,16,256]{2,1,0:T(8,128)S(1)}, u32[]{:S(2)}, u32[]{:S(2)}) async-start(f32[32,16,256]{2,1,0:T(8,128)} %bitcast.6), calls=%async_computation | async-start | bytes 1048576 | tf_op jit(solution)/shard_map/all_to_all | solution.py:35
  37.1 22.6 %all-to-all-start.1 = ((f32[32,16,256]{2,1,0:T(8,128)}), f32[32,16,256]{2,1,0:T(8,128)}, u32[]{:S(2)}, u32[]{:S(2)}) async-start(f32[32,16,256]{2,1,0:T(8,128)} %broadcast_select_fusion.3), calls=%async_computation.1 | async-start | bytes 1048576 | tf_op jit(solution)/shard_map/all_to_all | solution.py:38
  41.5 17.1 %collective-permute-start = (f32[256,256]{1,0:T(8,128)S(1)}, f32[256,256]{1,0:T(8,128)}, u32[]{:S(2)}, u32[]{:S(2)}) collective-permute-start(f32[256,256]{1,0:T(8,128)S(1)} %slice.178), channel_id=1, source_target_pairs={{0,1},{1,2},{2,3},{3,4},{4,5},{5,6},{6,7},{8,9},{9,10},{10,11},{11... | collective-permute-start | bytes 786440 | tf_op jit(solution)/shard_map/ppermute | solution.py:14
  60.8 1.4 copy-start.6
  62.2 4.5 %copy-start = (f32[1536,256]{1,0:T(8,128)}, f32[1536,256]{1,0:T(8,128)S(1)}, u32[]{:S(2)}) copy-start(f32[1536,256]{1,0:T(8,128)S(1)} %fusion.24) | copy-start | bytes 4718596
  68.7 25.5 %all-to-all-start.2 = ((f32[32,16,256]{2,1,0:T(8,128)}), f32[32,16,256]{2,1,0:T(8,128)S(1)}, u32[]{:S(2)}, u32[]{:S(2)}) async-start(f32[32,16,256]{2,1,0:T(8,128)} %bitcast.12), calls=%async_computation.2 | async-start | bytes 1048576 | tf_op jit(solution)/shard_map/all_to_all | solution.py:35
  94.1 27.4 %slice-start = ((s8[4718592]{0:T(1024)(128)(4,1)}), s8[524288]{0:T(1024)(128)(4,1)S(1)}, s32[]{:S(2)}) async-start(s8[4718592]{0:T(1024)(128)(4,1)} %bitcast.95), calls=%async_computation.8 | async-start | bytes 1048576
  95.7 22.2 %all-to-all-start.3 = ((f32[32,16,256]{2,1,0:T(8,128)}), f32[32,16,256]{2,1,0:T(8,128)}, u32[]{:S(2)}, u32[]{:S(2)}) async-start(f32[32,16,256]{2,1,0:T(8,128)} %broadcast_select_fusion.2), calls=%async_computation.3 | async-start | bytes 1048576 | tf_op jit(solution)/shard_map/all_to_all | solution.py:38
  100.1 16.6 %collective-permute-start.1 = (f32[256,256]{1,0:T(8,128)S(1)}, f32[256,256]{1,0:T(8,128)S(1)}, u32[]{:S(2)}, u32[]{:S(2)}) collective-permute-start(f32[256,256]{1,0:T(8,128)S(1)} %slice.185), channel_id=1, source_target_pairs={{0,1},{1,2},{2,3},{3,4},{4,5},{5,6},{6,7},{8,9},{9,10},{10,11},{11... | collective-permute-start | bytes 786440 | tf_op jit(solution)/shard_map/ppermute | solution.py:14
  117.9 3.6 %slice-start.1 = ((s8[4718592]{0:T(1024)(128)(4,1)}), s8[4194304]{0:T(1024)(128)(4,1)S(1)}, s32[]{:S(2)}) async-start(s8[4718592]{0:T(1024)(128)(4,1)} %bitcast.95), calls=%async_computation.9 | async-start | bytes 8388608
  119.2 2.7 %copy-start.7 = (f32[1,1,1536,256]{3,2,1,0:T(8,128)S(1)}, f32[1,1,1536,256]{3,2,1,0:T(8,128)}, u32[]{:S(2)}) copy-start(f32[1,1,1536,256]{3,2,1,0:T(8,128)} %param.9) | copy-start | bytes 4718596
  123.4 1.4 copy-start.4
  125.6 24.0 %all-to-all-start.4 = ((f32[32,16,256]{2,1,0:T(8,128)}), f32[32,16,256]{2,1,0:T(8,128)S(1)}, u32[]{:S(2)}, u32[]{:S(2)}) async-start(f32[32,16,256]{2,1,0:T(8,128)} %bitcast.18), calls=%async_computation.4 | async-start | bytes 1048576 | tf_op jit(solution)/shard_map/all_to_all | solution.py:35
  149.5 28.8 %slice-start.2 = ((s8[4718592]{0:T(1024)(128)(4,1)}), s8[524288]{0:T(1024)(128)(4,1)S(1)}, s32[]{:S(2)}) async-start(s8[4718592]{0:T(1024)(128)(4,1)} %bitcast.97), calls=%async_computation.10 | async-start | bytes 1048576
  152.9 22.2 %all-to-all-start.5 = ((f32[32,16,256]{2,1,0:T(8,128)}), f32[32,16,256]{2,1,0:T(8,128)}, u32[]{:S(2)}, u32[]{:S(2)}) async-start(f32[32,16,256]{2,1,0:T(8,128)} %broadcast_select_fusion.1), calls=%async_computation.5 | async-start | bytes 1048576 | tf_op jit(solution)/shard_map/all_to_all | solution.py:38
  157.3 2.7 %copy-start.12 = (f32[256,256]{1,0:T(8,128)}, f32[256,256]{1,0:T(8,128)S(1)}, u32[]{:S(2)}) copy-start(f32[256,256]{1,0:T(8,128)S(1)} %slice.193) | copy-start | bytes 786436
  157.3 15.9 %collective-permute-start.2 = (f32[256,256]{1,0:T(8,128)S(1)}, f32[256,256]{1,0:T(8,128)S(1)}, u32[]{:S(2)}, u32[]{:S(2)}) collective-permute-start(f32[256,256]{1,0:T(8,128)S(1)} %slice.193), channel_id=1, source_target_pairs={{0,1},{1,2},{2,3},{3,4},{4,5},{5,6},{6,7},{8,9},{9,10},{10,11},{11... | collective-permute-start | bytes 786440 | tf_op jit(solution)/shard_map/ppermute | solution.py:14
  161.1 15.3 %copy-start.10 = (f32[512,256]{1,0:T(8,128)}, f32[512,256]{1,0:T(8,128)S(1)}, u32[]{:S(2)}) copy-start(f32[512,256]{1,0:T(8,128)S(1)} %slice.197) | copy-start | bytes 1572868
  175.1 1.6 copy-start.5
  175.1 3.3 %slice-start.3 = ((s8[4718592]{0:T(1024)(128)(4,1)}), s8[4194304]{0:T(1024)(128)(4,1)S(1)}, s32[]{:S(2)}) async-start(s8[4718592]{0:T(1024)(128)(4,1)} %bitcast.97), calls=%async_computation.11 | async-start | bytes 8388608
  176.7 2.1 copy-start.8
  176.7 2.1 copy-start.11
  176.7 2.2 copy-start.13
  178.9 2.8 %copy-start.1 = (f32[1536,256]{1,0:T(8,128)}, f32[1536,256]{1,0:T(8,128)S(1)}, u32[]{:S(2)}) copy-start(f32[1536,256]{1,0:T(8,128)S(1)} %add_subtract_fusion) | copy-start | bytes 4718596
  183.1 35.9 %copy-start.9 = (f32[768,256]{1,0:T(8,128)}, f32[768,256]{1,0:T(8,128)S(1)}, u32[]{:S(2)}) copy-start(f32[768,256]{1,0:T(8,128)S(1)} %get-tuple-element.15) | copy-start | bytes 2359300
  183.9 24.6 %all-to-all-start.6 = ((f32[32,16,256]{2,1,0:T(8,128)}), f32[32,16,256]{2,1,0:T(8,128)S(1)}, u32[]{:S(2)}, u32[]{:S(2)}) async-start(f32[32,16,256]{2,1,0:T(8,128)} %bitcast.99), calls=%async_computation.6 | async-start | bytes 1048576 | tf_op jit(solution)/shard_map/all_to_all | solution.py:35
  211.9 22.2 %all-to-all-start.7 = ((f32[32,16,256]{2,1,0:T(8,128)}), f32[32,16,256]{2,1,0:T(8,128)}, u32[]{:S(2)}, u32[]{:S(2)}) async-start(f32[32,16,256]{2,1,0:T(8,128)} %broadcast_select_fusion), calls=%async_computation.7 | async-start | bytes 1048576 | tf_op jit(solution)/shard_map/all_to_all | solution.py:38
  216.4 4.6 %copy-start.15 = (f32[256,256]{1,0:T(8,128)}, f32[256,256]{1,0:T(8,128)S(1)}, u32[]{:S(2)}) copy-start(f32[256,256]{1,0:T(8,128)S(1)} %slice.201) | copy-start | bytes 786436
  216.4 14.5 %collective-permute-start.3 = (f32[256,256]{1,0:T(8,128)S(1)}, f32[256,256]{1,0:T(8,128)S(1)}, u32[]{:S(2)}, u32[]{:S(2)}) collective-permute-start(f32[256,256]{1,0:T(8,128)S(1)} %slice.201), channel_id=1, source_target_pairs={{0,1},{1,2},{2,3},{3,4},{4,5},{5,6},{6,7},{8,9},{9,10},{10,11},{11... | collective-permute-start | bytes 786440 | tf_op jit(solution)/shard_map/ppermute | solution.py:14
  218.9 16.6 %copy-start.2 = (f32[1536,256]{1,0:T(8,128)S(1)}, f32[1536,256]{1,0:T(8,128)}, u32[]{:S(2)}) copy-start(f32[1536,256]{1,0:T(8,128)} %copy-done.1) | copy-start | bytes 4718596
  234.1 1.4 copy-start.16
  (2 other events, 2.5 us)
where the time goes:
time: 239 us; the launch traced here: 238 us
  waiting for transfers between devices  112 us (47%)
  starting transfers between devices  58.1 us (24%)
  other arithmetic  25.3 us (11%)
  local copies, waits for them, and re-layouts  18.2 us (8%)
  matrix products  12.9 us (5%)
  between operations  10.7 us (4%)
    all_to_all x4, waiting for transfers between devices, local(): lax.all_to_all(couple, 'area', split_axis=0, concat_axis=0, tiled=True)  70.6 us
    ppermute x4, waiting for transfers between devices, from_behind(): return lax.ppermute(array, axis, pairs)  38.1 us
    all_to_all x4, starting transfers between devices, local(): lax.all_to_all(couple, 'area', split_axis=0, concat_axis=0, tiled=True)  31.1 us
    all_to_all x4, starting transfers between devices, local(): lax.all_to_all(pieces.reshape(COUPLE, couple.shape[1]), 'area', split_axi...  17.7 us
    dot_general x4, matrix products, local(): x_full = jnp.dot(matrix, v_now, preferred_element_type=jnp.float32)  12.9 us
    ppermute x4, starting transfers between devices, from_behind(): return lax.ppermute(array, axis, pairs)  9.34 us
    select_n x4, other arithmetic, local(): pieces = jnp.take(pieces, row, axis=0)  5.74 us
    add x4, other arithmetic, local(): new_couple = couple + linked * 0.5 * (other - couple)  4.98 us
  transfers between devices with their start and end apart: 12, of which 11 were waited for; matrix products, arithmetic and copies ran while one was open for 5% of the time, Pallas kernels for 0%

commit v1 on v0

v1 whole, which is shorter than its diff:
```python
import jax
import jax.numpy as jnp
from jax import lax
from jax.sharding import PartitionSpec as P

COUPLE = 512
BOUND = 256
ITERS = 4


def from_behind(array, axis, by):
    length = lax.axis_size(axis)
    pairs = [(i, i + by) for i in range(length) if 0 <= i + by < length]
    return lax.ppermute(array, axis, pairs)


def exchange(array, colour, axis):
    length = lax.axis_size(axis)

    def swap(bits):
        pairs = [(i, i ^ bits) for i in range(length)]
        return lambda block: lax.ppermute(block, axis, pairs)

    return lax.switch(colour - 1, [swap(bits) for bits in range(1, length)], array)


def local(kkt, offsets, lower, upper, partners, adjacency):
    matrix = kkt[0, 0]
    costs = offsets[0, 0]
    low = lower[0, 0][:, None]
    high = upper[0, 0][:, None]
    sent = COUPLE + BOUND
    area = lax.axis_index("area")

    def iterate(step, carry):
        z_now, u_now = carry
        v_now = (costs + z_now - u_now).astype(jnp.bfloat16)
        x_head = jnp.dot(matrix[:sent], v_now, preferred_element_type=jnp.float32)
        y_head = jnp.minimum(jnp.maximum(x_head + u_now[:sent], low[:sent]), high[:sent])
        couple = y_head[:COUPLE]
        ends = y_head[COUPLE:sent]
        before = from_behind(ends, "win", 1)
        row = partners[step]
        other = exchange(couple, row[0], "area")
        linked = (adjacency[area, row[area]] == 1).astype(couple.dtype)
        new_couple = couple + linked * 0.5 * (other - couple)
        x_tail = jnp.dot(matrix[sent:], v_now, preferred_element_type=jnp.float32)
        y_tail = jnp.minimum(jnp.maximum(x_tail + u_now[sent:], low[sent:]), high[sent:])
        starts = 0.5 * (y_tail[:BOUND] + before)
        z_next = jnp.concatenate([new_couple, ends, starts, y_tail[BOUND:]], axis=0)
        x_full = jnp.concatenate([x_head, x_tail], axis=0)
        return z_next, u_now + x_full - z_next

    z_now, u_now = lax.fori_loop(0, ITERS, iterate, (jnp.zeros_like(costs), jnp.zeros_like(costs)))
    return (z_now[None, None], u_now[None, None])


def solution(mesh):
    in_specs = (
        P("area", "win", None, None),
        P("area", "win", None, None),
        P("area", "win", None),
        P("area", "win", None),
        P(),
        P(),
    )
    out_specs = (P("area", "win", None, None), P("area", "win", None, None))
    return jax.shard_map(local, mesh=mesh, in_specs=in_specs, out_specs=out_specs, check_vma=False)
```

time: 239 us -> 164 us (0.69)
  the two profiles are of different devices: /device:TPU:24 before, /device:TPU:33 now
where the time goes in v1:
time: 164 us; the launch traced here: 163 us
  waiting for transfers between devices  48.8 us (30%)
  local copies, waits for them, and re-layouts  33.1 us (20%)
  starting transfers between devices  30.5 us (19%)
  other arithmetic  28.8 us (18%)
  matrix products  11.1 us (7%)
  loops' own time  10 us (6%)
    ppermute x4, waiting for transfers between devices, swap(): return lambda block: lax.ppermute(block, axis, pairs)  48.8 us
    ppermute x4, starting transfers between devices, swap(): return lambda block: lax.ppermute(block, axis, pairs)  16.5 us
    ppermute x4, starting transfers between devices, from_behind(): return lax.ppermute(array, axis, pairs)  13.9 us
    sub x4, other arithmetic, iterate(): return (z_next, u_now + x_full - z_next)  12 us
    convert_element_type x4, other arithmetic, iterate(): v_now = (costs + z_now - u_now).astype(jnp.bfloat16)  11.7 us
    another operation x1, loops' own time, local(): lax.fori_loop(0, ITERS, iterate, (jnp.zeros_like(costs), jnp.zeros_like(c...  9.71 us
    dot_general x4, matrix products, iterate(): x_head = jnp.dot(matrix[:sent], v_now, preferred_element_type=jnp.float32)  7.96 us
    dynamic_slice x8, local copies, waits for them, and re-layouts, iterate(): linked = (adjacency[area, row[area]] == 1).astype(couple.dtype)  7.49 us
  transfers between devices with their start and end apart: 8, of which 4 were waited for; matrix products, arithmetic and copies ran while one was open for 10% of the time, Pallas kernels for 0%

profile of v1, /device:TPU:33, one launch (start us, length us, event | category | flops | bytes accessed | tf_op | source)
XLA Modules:
  0.0 163.0 jit_solution(6194970211461060820)
XLA Ops:
  0.6 3.0 %copy.40 = f32[1,1,1536,256]{2,3,1,0:T(8,128)} copy(f32[1,1,1536,256]{3,2,1,0:T(8,128)} %param.40) | data formatting | bytes 3145728 | tf_op args[1]
  5.0 153.2 %while.19 = (s32[]{:T(128)}, f32[1536,256]{0,1:T(8,128)}, f32[1536,256]{0,1:T(8,128)}, f32[1536,256]{0,1:T(8,128)}, bf16[1536,1536]{1,0:T(8,128)(2,1)}, /*index=...) while((s32[]{:T(128)}, f32[1536,256]{0,1:T(8,128)}, ...), condition=%wide.region_32.0_spmd.clone, body=%wide.region_0.0_spmd.clone.sunk | while | flops 1213595648 | bytes 67412792 | solution.py:54
  5.1 2.6 %subtract_convert_fusion.2 = (bf16[1536,256]{0,1:T(8,128)(2,1)S(1)}, f32[1536,256]{0,1:T(8,128)S(1)}) fusion(f32[1536,256]{0,1:T(8,128)} %get-tuple-element.637, f32[1536,256]{0,1:T(8,128)} %get-tuple-element.614, f32[1536,256]{0,1:T(8,128)} %get-tuple-element.615, pred[]{:T(512)S(6)} %compare.3), kind=kLoop, calls=%fused_computation.7.clone.1 | loop fusion | flops 1572864 | bytes 7077889 | tf_op jit(solution)/shard_map/while/body/eval_jaxpr/convert_element_type | solution.py:37
  9.2 2.0 %fusion.29 = (f32[768,256]{0,1:T(8,128)S(1)}, f32[768,256]{0,1:T(8,128)}, f32[768,256]{0,1:T(8,128)}) fusion(f32[1536,256]{0,1:T(8,128)S(1)} %get-tuple-element.549, f32[768]{0:T(1024)S(1)} %get-tuple-element.551, f32[768]{0:T(1024)S(1)} %get-tuple-element.552, f32[768]{0:T(1024)S(1)} %get-tuple-element.553, f32[768]{0:T(1024)S(1)} %get-tuple-element.554, ...), kind=kOutput, calls=%fused_computation.15.clone.1 | convolution fusion | flops 605159424 | bytes 7880704 | tf_op jit(solution)/shard_map/while/body/eval_jaxpr/dot_general | solution.py:38
  11.9 3.8 %collective-permute-start.31 = (f32[256,256]{0,1:T(8,128)}, f32[256,256]{0,1:T(8,128)}, u32[]{:S(2)}, u32[]{:S(2)}) collective-permute-start(f32[256,256]{0,1:T(8,128)} %slice.300), channel_id=1, source_target_pairs={{0,1},{1,2},{2,3},{3,4},{4,5},{5,6},{6,7},{8,9},{9,10},{10,11},{11... | collective-permute-start | bytes 786440 | tf_op jit(solution)/shard_map/while/body/eval_jaxpr/ppermute | solution.py:14
  17.5 1.9 %slice.299 = f32[512,256]{0,1:T(8,128)} slice(f32[768,256]{0,1:T(8,128)} %get-tuple-element.556), slice={[256:768], [0:256]} | slice | bytes 1048576 | tf_op jit(solution)/shard_map/while/body/eval_jaxpr/slice | solution.py:50
  21.8 31.2 %conditional.3 = (f32[512,256]{0,1:T(8,128)S(1)}) conditional(s32[]{:T(128)} %bitcast.27, (f32[512,256]{0,1:T(8,128)S(1)}) %tuple.197, (f32[512,256]{0,1:T(8,128)S(1)}) %tuple.197, (f32[512,256]{0,1:T(8,128)S(1)}) %tuple.197, (f32[512,256]{0,1:T(8,128)S(1)}) %tuple.197, (f32[512,256]{0,1:T(8,128)S(1)}) %tuple.197, ...), branch_computations={%region_1.0_spmd, %region_2.0_spmd, %region_3.0_spmd, %region_4.0_... | conditional | bytes 4194352 | solution.py:24
  22.1 7.9 %collective-permute-start.18 = (f32[512,256]{1,0:T(8,128)S(1)}, f32[512,256]{1,0:T(8,128)S(1)}, u32[]{:S(2)}, u32[]{:S(2)}) collective-permute-start(f32[512,256]{1,0:T(8,128)S(1)} %copy.92), channel_id=1, source_target_pairs={{0,152},{8,144},{16,136},{24,128},{32,184},{40,176},{48,168},{56,1... | collective-permute-start | bytes 1572872 | tf_op jit(solution)/shard_map/while/body/eval_jaxpr/cond/branch_18_fun/ppermute | solution.py:22
  30.0 22.8 %collective-permute-done.18 = f32[512,256]{1,0:T(8,128)S(1)} collective-permute-done((f32[512,256]{1,0:T(8,128)S(1)}, f32[512,256]{1,0:T(8,128)S(1)}, u32[]{:S(2)}, u32[]{:S(2)}) %collective-permute-start.18) | collective-permute-done | bytes 524320 | tf_op jit(solution)/shard_map/while/body/eval_jaxpr/cond/branch_18_fun/ppermute | solution.py:22
  54.7 3.0 %fusion.31 = (f32[1536,256]{0,1:T(8,128)}, f32[1536,256]{0,1:T(8,128)}) fusion(f32[1536,256]{0,1:T(8,128)S(1)} %get-tuple-element.549, f32[768,256]{0,1:T(8,128)S(1)} %copy-done.1, f32[768,256]{0,1:T(8,128)S(1)} %copy-done.2, f32[512,256]{0,1:T(8,128)S(1)} %copy-done.4, f32[256,256]{0,1:T(8,128)S(1)} %fusion.30, f32[256,256]{0,1:T(8,128)} %slice.300, ...), kind=kLoop, calls=%fused_computation.6.clone.1 | loop fusion | flops 2359296 | bytes 7864320 | tf_op jit(solution)/shard_map/while/body/eval_jaxpr/sub | solution.py:52
  57.8 3.0 %subtract_convert_fusion.2 = (bf16[1536,256]{0,1:T(8,128)(2,1)S(1)}, f32[1536,256]{0,1:T(8,128)S(1)}) fusion(f32[1536,256]{0,1:T(8,128)} %get-tuple-element.637, f32[1536,256]{0,1:T(8,128)} %get-tuple-element.614, f32[1536,256]{0,1:T(8,128)} %get-tuple-element.615, pred[]{:T(512)S(6)} %compare.3), kind=kLoop, calls=%fused_computation.7.clone.1 | loop fusion | flops 1572864 | bytes 7077889 | tf_op jit(solution)/shard_map/while/body/eval_jaxpr/convert_element_type | solution.py:37
  62.4 2.0 %fusion.29 = (f32[768,256]{0,1:T(8,128)S(1)}, f32[768,256]{0,1:T(8,128)}, f32[768,256]{0,1:T(8,128)}) fusion(f32[1536,256]{0,1:T(8,128)S(1)} %get-tuple-element.549, f32[768]{0:T(1024)S(1)} %get-tuple-element.551, f32[768]{0:T(1024)S(1)} %get-tuple-element.552, f32[768]{0:T(1024)S(1)} %get-tuple-element.553, f32[768]{0:T(1024)S(1)} %get-tuple-element.554, ...), kind=kOutput, calls=%fused_computation.15.clone.1 | convolution fusion | flops 605159424 | bytes 7880704 | tf_op jit(solution)/shard_map/while/body/eval_jaxpr/dot_general | solution.py:38
  65.1 3.1 %collective-permute-start.31 = (f32[256,256]{0,1:T(8,128)}, f32[256,256]{0,1:T(8,128)}, u32[]{:S(2)}, u32[]{:S(2)}) collective-permute-start(f32[256,256]{0,1:T(8,128)} %slice.300), channel_id=1, source_target_pairs={{0,1},{1,2},{2,3},{3,4},{4,5},{5,6},{6,7},{8,9},{9,10},{10,11},{11... | collective-permute-start | bytes 786440 | tf_op jit(solution)/shard_map/while/body/eval_jaxpr/ppermute | solution.py:14
  70.0 1.9 %slice.299 = f32[512,256]{0,1:T(8,128)} slice(f32[768,256]{0,1:T(8,128)} %get-tuple-element.556), slice={[256:768], [0:256]} | slice | bytes 1048576 | tf_op jit(solution)/shard_map/while/body/eval_jaxpr/slice | solution.py:50
  74.3 2.5 %conditional.3 = (f32[512,256]{0,1:T(8,128)S(1)}) conditional(s32[]{:T(128)} %bitcast.27, (f32[512,256]{0,1:T(8,128)S(1)}) %tuple.197, (f32[512,256]{0,1:T(8,128)S(1)}) %tuple.197, (f32[512,256]{0,1:T(8,128)S(1)}) %tuple.197, (f32[512,256]{0,1:T(8,128)S(1)}) %tuple.197, (f32[512,256]{0,1:T(8,128)S(1)}) %tuple.197, ...), branch_computations={%region_1.0_spmd, %region_2.0_spmd, %region_3.0_spmd, %region_4.0_... | conditional | bytes 4194352 | solution.py:24
  78.4 3.0 %fusion.31 = (f32[1536,256]{0,1:T(8,128)}, f32[1536,256]{0,1:T(8,128)}) fusion(f32[1536,256]{0,1:T(8,128)S(1)} %get-tuple-element.549, f32[768,256]{0,1:T(8,128)S(1)} %copy-done.1, f32[768,256]{0,1:T(8,128)S(1)} %copy-done.2, f32[512,256]{0,1:T(8,128)S(1)} %copy-done.4, f32[256,256]{0,1:T(8,128)S(1)} %fusion.30, f32[256,256]{0,1:T(8,128)} %slice.300, ...), kind=kLoop, calls=%fused_computation.6.clone.1 | loop fusion | flops 2359296 | bytes 7864320 | tf_op jit(solution)/shard_map/while/body/eval_jaxpr/sub | solution.py:52
  81.5 3.0 %subtract_convert_fusion.2 = (bf16[1536,256]{0,1:T(8,128)(2,1)S(1)}, f32[1536,256]{0,1:T(8,128)S(1)}) fusion(f32[1536,256]{0,1:T(8,128)} %get-tuple-element.637, f32[1536,256]{0,1:T(8,128)} %get-tuple-element.614, f32[1536,256]{0,1:T(8,128)} %get-tuple-element.615, pred[]{:T(512)S(6)} %compare.3), kind=kLoop, calls=%fused_computation.7.clone.1 | loop fusion | flops 1572864 | bytes 7077889 | tf_op jit(solution)/shard_map/while/body/eval_jaxpr/convert_element_type | solution.py:37
  86.1 2.0 %fusion.29 = (f32[768,256]{0,1:T(8,128)S(1)}, f32[768,256]{0,1:T(8,128)}, f32[768,256]{0,1:T(8,128)}) fusion(f32[1536,256]{0,1:T(8,128)S(1)} %get-tuple-element.549, f32[768]{0:T(1024)S(1)} %get-tuple-element.551, f32[768]{0:T(1024)S(1)} %get-tuple-element.552, f32[768]{0:T(1024)S(1)} %get-tuple-element.553, f32[768]{0:T(1024)S(1)} %get-tuple-element.554, ...), kind=kOutput, calls=%fused_computation.15.clone.1 | convolution fusion | flops 605159424 | bytes 7880704 | tf_op jit(solution)/shard_map/while/body/eval_jaxpr/dot_general | solution.py:38
  88.8 2.8 %collective-permute-start.31 = (f32[256,256]{0,1:T(8,128)}, f32[256,256]{0,1:T(8,128)}, u32[]{:S(2)}, u32[]{:S(2)}) collective-permute-start(f32[256,256]{0,1:T(8,128)} %slice.300), channel_id=1, source_target_pairs={{0,1},{1,2},{2,3},{3,4},{4,5},{5,6},{6,7},{8,9},{9,10},{10,11},{11... | collective-permute-start | bytes 786440 | tf_op jit(solution)/shard_map/while/body/eval_jaxpr/ppermute | solution.py:14
  93.4 1.9 %slice.299 = f32[512,256]{0,1:T(8,128)} slice(f32[768,256]{0,1:T(8,128)} %get-tuple-element.556), slice={[256:768], [0:256]} | slice | bytes 1048576 | tf_op jit(solution)/shard_map/while/body/eval_jaxpr/slice | solution.py:50
  97.7 30.7 %conditional.3 = (f32[512,256]{0,1:T(8,128)S(1)}) conditional(s32[]{:T(128)} %bitcast.27, (f32[512,256]{0,1:T(8,128)S(1)}) %tuple.197, (f32[512,256]{0,1:T(8,128)S(1)}) %tuple.197, (f32[512,256]{0,1:T(8,128)S(1)}) %tuple.197, (f32[512,256]{0,1:T(8,128)S(1)}) %tuple.197, (f32[512,256]{0,1:T(8,128)S(1)}) %tuple.197, ...), branch_computations={%region_1.0_spmd, %region_2.0_spmd, %region_3.0_spmd, %region_4.0_... | conditional | bytes 4194352 | solution.py:24
  98.0 7.4 %collective-permute-start.22 = (f32[512,256]{1,0:T(8,128)S(1)}, f32[512,256]{1,0:T(8,128)S(1)}, u32[]{:S(2)}, u32[]{:S(2)}) collective-permute-start(f32[512,256]{1,0:T(8,128)S(1)} %copy.96), channel_id=1, source_target_pairs={{0,184},{8,176},{16,168},{24,160},{32,152},{40,144},{48,136},{56,1... | collective-permute-start | bytes 1572872 | tf_op jit(solution)/shard_map/while/body/eval_jaxpr/cond/branch_22_fun/ppermute | solution.py:22
  105.4 22.8 %collective-permute-done.22 = f32[512,256]{1,0:T(8,128)S(1)} collective-permute-done((f32[512,256]{1,0:T(8,128)S(1)}, f32[512,256]{1,0:T(8,128)S(1)}, u32[]{:S(2)}, u32[]{:S(2)}) %collective-permute-start.22) | collective-permute-done | bytes 524320 | tf_op jit(solution)/shard_map/while/body/eval_jaxpr/cond/branch_22_fun/ppermute | solution.py:22
  130.1 3.0 %fusion.31 = (f32[1536,256]{0,1:T(8,128)}, f32[1536,256]{0,1:T(8,128)}) fusion(f32[1536,256]{0,1:T(8,128)S(1)} %get-tuple-element.549, f32[768,256]{0,1:T(8,128)S(1)} %copy-done.1, f32[768,256]{0,1:T(8,128)S(1)} %copy-done.2, f32[512,256]{0,1:T(8,128)S(1)} %copy-done.4, f32[256,256]{0,1:T(8,128)S(1)} %fusion.30, f32[256,256]{0,1:T(8,128)} %slice.300, ...), kind=kLoop, calls=%fused_computation.6.clone.1 | loop fusion | flops 2359296 | bytes 7864320 | tf_op jit(solution)/shard_map/while/body/eval_jaxpr/sub | solution.py:52
  133.2 3.0 %subtract_convert_fusion.2 = (bf16[1536,256]{0,1:T(8,128)(2,1)S(1)}, f32[1536,256]{0,1:T(8,128)S(1)}) fusion(f32[1536,256]{0,1:T(8,128)} %get-tuple-element.637, f32[1536,256]{0,1:T(8,128)} %get-tuple-element.614, f32[1536,256]{0,1:T(8,128)} %get-tuple-element.615, pred[]{:T(512)S(6)} %compare.3), kind=kLoop, calls=%fused_computation.7.clone.1 | loop fusion | flops 1572864 | bytes 7077889 | tf_op jit(solution)/shard_map/while/body/eval_jaxpr/convert_element_type | solution.py:37
  137.8 2.0 %fusion.29 = (f32[768,256]{0,1:T(8,128)S(1)}, f32[768,256]{0,1:T(8,128)}, f32[768,256]{0,1:T(8,128)}) fusion(f32[1536,256]{0,1:T(8,128)S(1)} %get-tuple-element.549, f32[768]{0:T(1024)S(1)} %get-tuple-element.551, f32[768]{0:T(1024)S(1)} %get-tuple-element.552, f32[768]{0:T(1024)S(1)} %get-tuple-element.553, f32[768]{0:T(1024)S(1)} %get-tuple-element.554, ...), kind=kOutput, calls=%fused_computation.15.clone.1 | convolution fusion | flops 605159424 | bytes 7880704 | tf_op jit(solution)/shard_map/while/body/eval_jaxpr/dot_general | solution.py:38
  140.5 4.2 %collective-permute-start.31 = (f32[256,256]{0,1:T(8,128)}, f32[256,256]{0,1:T(8,128)}, u32[]{:S(2)}, u32[]{:S(2)}) collective-permute-start(f32[256,256]{0,1:T(8,128)} %slice.300), channel_id=1, source_target_pairs={{0,1},{1,2},{2,3},{3,4},{4,5},{5,6},{6,7},{8,9},{9,10},{10,11},{11... | collective-permute-start | bytes 786440 | tf_op jit(solution)/shard_map/while/body/eval_jaxpr/ppermute | solution.py:14
  146.4 1.9 %slice.299 = f32[512,256]{0,1:T(8,128)} slice(f32[768,256]{0,1:T(8,128)} %get-tuple-element.556), slice={[256:768], [0:256]} | slice | bytes 1048576 | tf_op jit(solution)/shard_map/while/body/eval_jaxpr/slice | solution.py:50
  150.8 2.8 %conditional.3 = (f32[512,256]{0,1:T(8,128)S(1)}) conditional(s32[]{:T(128)} %bitcast.27, (f32[512,256]{0,1:T(8,128)S(1)}) %tuple.197, (f32[512,256]{0,1:T(8,128)S(1)}) %tuple.197, (f32[512,256]{0,1:T(8,128)S(1)}) %tuple.197, (f32[512,256]{0,1:T(8,128)S(1)}) %tuple.197, (f32[512,256]{0,1:T(8,128)S(1)}) %tuple.197, ...), branch_computations={%region_1.0_spmd, %region_2.0_spmd, %region_3.0_spmd, %region_4.0_... | conditional | bytes 4194352 | solution.py:24
  155.2 3.0 %fusion.31 = (f32[1536,256]{0,1:T(8,128)}, f32[1536,256]{0,1:T(8,128)}) fusion(f32[1536,256]{0,1:T(8,128)S(1)} %get-tuple-element.549, f32[768,256]{0,1:T(8,128)S(1)} %copy-done.1, f32[768,256]{0,1:T(8,128)S(1)} %copy-done.2, f32[512,256]{0,1:T(8,128)S(1)} %copy-done.4, f32[256,256]{0,1:T(8,128)S(1)} %fusion.30, f32[256,256]{0,1:T(8,128)} %slice.300, ...), kind=kLoop, calls=%fused_computation.6.clone.1 | loop fusion | flops 2359296 | bytes 7864320 | tf_op jit(solution)/shard_map/while/body/eval_jaxpr/sub | solution.py:52
  158.2 3.1 %copy.42 = f32[1536,256]{1,0:T(8,128)} copy(f32[1536,256]{0,1:T(8,128)} %get-tuple-element.366) | data formatting | bytes 3145728 | tf_op jit(solution)/shard_map/while | solution.py:54
  161.4 1.6 copy.41
  (102 shorter events, 30.4 us)
Async XLA Ops:
  3.7 1.3 copy-start.6
  3.7 1.3 copy-start.7
  3.7 1.3 copy-start.8
  5.1 3.3 %copy-start.5 = (bf16[1536,1536]{1,0:T(8,128)(2,1)S(1)}, bf16[1536,1536]{1,0:T(8,128)(2,1)}, u32[]{:S(2)}) copy-start(bf16[1536,1536]{1,0:T(8,128)(2,1)} %get-tuple-element.638) | copy-start | bytes 14155780 | tf_op jit(solution)/shard_map/while
  9.1 2.0 %copy-start = (f32[768,256]{0,1:T(8,128)}, f32[768,256]{0,1:T(8,128)S(1)}, u32[]{:S(2)}) copy-start(f32[768,256]{0,1:T(8,128)S(1)} %fusion.28) | copy-start | bytes 2359300 | tf_op jit(solution)/shard_map/while
  11.9 41.3 %collective-permute-start.31 = (f32[256,256]{0,1:T(8,128)}, f32[256,256]{0,1:T(8,128)}, u32[]{:S(2)}, u32[]{:S(2)}) collective-permute-start(f32[256,256]{0,1:T(8,128)} %slice.300), channel_id=1, source_target_pairs={{0,1},{1,2},{2,3},{3,4},{4,5},{5,6},{6,7},{8,9},{9,10},{10,11},{11... | collective-permute-start | bytes 786440 | tf_op jit(solution)/shard_map/while/body/eval_jaxpr/ppermute | solution.py:14
  22.1 30.8 %collective-permute-start.18 = (f32[512,256]{1,0:T(8,128)S(1)}, f32[512,256]{1,0:T(8,128)S(1)}, u32[]{:S(2)}, u32[]{:S(2)}) collective-permute-start(f32[512,256]{1,0:T(8,128)S(1)} %copy.92), channel_id=1, source_target_pairs={{0,152},{8,144},{16,136},{24,128},{32,184},{40,176},{48,168},{56,1... | collective-permute-start | bytes 1572872 | tf_op jit(solution)/shard_map/while/body/eval_jaxpr/cond/branch_18_fun/ppermute | solution.py:22
  53.1 1.3 copy-start.1
  53.1 1.5 copy-start.2
  53.1 1.7 %copy-start.4 = (f32[512,256]{0,1:T(8,128)S(1)}, f32[512,256]{0,1:T(8,128)}, u32[]{:S(2)}) copy-start(f32[512,256]{0,1:T(8,128)} %slice.299) | copy-start | bytes 1572868 | tf_op jit(solution)/shard_map/while
  57.8 3.8 %copy-start.5 = (bf16[1536,1536]{1,0:T(8,128)(2,1)S(1)}, bf16[1536,1536]{1,0:T(8,128)(2,1)}, u32[]{:S(2)}) copy-start(bf16[1536,1536]{1,0:T(8,128)(2,1)} %get-tuple-element.638) | copy-start | bytes 14155780 | tf_op jit(solution)/shard_map/while
  62.3 2.0 %copy-start = (f32[768,256]{0,1:T(8,128)}, f32[768,256]{0,1:T(8,128)S(1)}, u32[]{:S(2)}) copy-start(f32[768,256]{0,1:T(8,128)S(1)} %fusion.28) | copy-start | bytes 2359300 | tf_op jit(solution)/shard_map/while
  65.1 11.8 %collective-permute-start.31 = (f32[256,256]{0,1:T(8,128)}, f32[256,256]{0,1:T(8,128)}, u32[]{:S(2)}, u32[]{:S(2)}) collective-permute-start(f32[256,256]{0,1:T(8,128)} %slice.300), channel_id=1, source_target_pairs={{0,1},{1,2},{2,3},{3,4},{4,5},{5,6},{6,7},{8,9},{9,10},{10,11},{11... | collective-permute-start | bytes 786440 | tf_op jit(solution)/shard_map/while/body/eval_jaxpr/ppermute | solution.py:14
  74.5 2.0 %collective-permute-start = (f32[512,256]{1,0:T(8,128)S(1)}, f32[512,256]{1,0:T(8,128)S(1)}, u32[]{:S(2)}, u32[]{:S(2)}) collective-permute-start(f32[512,256]{1,0:T(8,128)S(1)} %copy.74), channel_id=1, source_target_pairs={{0,8},{8,0},{16,24},{24,16},{32,40},{40,32},{48,56},{56,48},{64,72... | collective-permute-start | bytes 1572872 | tf_op jit(solution)/shard_map/while/body/eval_jaxpr/cond/branch_0_fun/ppermute | solution.py:22
  76.8 1.3 copy-start.1
  76.8 1.5 copy-start.2
  76.8 1.7 %copy-start.4 = (f32[512,256]{0,1:T(8,128)S(1)}, f32[512,256]{0,1:T(8,128)}, u32[]{:S(2)}) copy-start(f32[512,256]{0,1:T(8,128)} %slice.299) | copy-start | bytes 1572868 | tf_op jit(solution)/shard_map/while
  81.5 3.8 %copy-start.5 = (bf16[1536,1536]{1,0:T(8,128)(2,1)S(1)}, bf16[1536,1536]{1,0:T(8,128)(2,1)}, u32[]{:S(2)}) copy-start(bf16[1536,1536]{1,0:T(8,128)(2,1)} %get-tuple-element.638) | copy-start | bytes 14155780 | tf_op jit(solution)/shard_map/while
  86.1 2.0 %copy-start = (f32[768,256]{0,1:T(8,128)}, f32[768,256]{0,1:T(8,128)S(1)}, u32[]{:S(2)}) copy-start(f32[768,256]{0,1:T(8,128)S(1)} %fusion.28) | copy-start | bytes 2359300 | tf_op jit(solution)/shard_map/while
  88.8 39.8 %collective-permute-start.31 = (f32[256,256]{0,1:T(8,128)}, f32[256,256]{0,1:T(8,128)}, u32[]{:S(2)}, u32[]{:S(2)}) collective-permute-start(f32[256,256]{0,1:T(8,128)} %slice.300), channel_id=1, source_target_pairs={{0,1},{1,2},{2,3},{3,4},{4,5},{5,6},{6,7},{8,9},{9,10},{10,11},{11... | collective-permute-start | bytes 786440 | tf_op jit(solution)/shard_map/while/body/eval_jaxpr/ppermute | solution.py:14
  98.0 30.3 %collective-permute-start.22 = (f32[512,256]{1,0:T(8,128)S(1)}, f32[512,256]{1,0:T(8,128)S(1)}, u32[]{:S(2)}, u32[]{:S(2)}) collective-permute-start(f32[512,256]{1,0:T(8,128)S(1)} %copy.96), channel_id=1, source_target_pairs={{0,184},{8,176},{16,168},{24,160},{32,152},{40,144},{48,136},{56,1... | collective-permute-start | bytes 1572872 | tf_op jit(solution)/shard_map/while/body/eval_jaxpr/cond/branch_22_fun/ppermute | solution.py:22
  128.5 1.3 copy-start.1
  128.5 1.5 copy-start.2
  128.5 1.7 %copy-start.4 = (f32[512,256]{0,1:T(8,128)S(1)}, f32[512,256]{0,1:T(8,128)}, u32[]{:S(2)}) copy-start(f32[512,256]{0,1:T(8,128)} %slice.299) | copy-start | bytes 1572868 | tf_op jit(solution)/shard_map/while
  133.2 3.8 %copy-start.5 = (bf16[1536,1536]{1,0:T(8,128)(2,1)S(1)}, bf16[1536,1536]{1,0:T(8,128)(2,1)}, u32[]{:S(2)}) copy-start(bf16[1536,1536]{1,0:T(8,128)(2,1)} %get-tuple-element.638) | copy-start | bytes 14155780 | tf_op jit(solution)/shard_map/while
  137.8 2.0 %copy-start = (f32[768,256]{0,1:T(8,128)}, f32[768,256]{0,1:T(8,128)S(1)}, u32[]{:S(2)}) copy-start(f32[768,256]{0,1:T(8,128)S(1)} %fusion.28) | copy-start | bytes 2359300 | tf_op jit(solution)/shard_map/while
  140.5 13.2 %collective-permute-start.31 = (f32[256,256]{0,1:T(8,128)}, f32[256,256]{0,1:T(8,128)}, u32[]{:S(2)}, u32[]{:S(2)}) collective-permute-start(f32[256,256]{0,1:T(8,128)} %slice.300), channel_id=1, source_target_pairs={{0,1},{1,2},{2,3},{3,4},{4,5},{5,6},{6,7},{8,9},{9,10},{10,11},{11... | collective-permute-start | bytes 786440 | tf_op jit(solution)/shard_map/while/body/eval_jaxpr/ppermute | solution.py:14
  151.0 2.3 %collective-permute-start = (f32[512,256]{1,0:T(8,128)S(1)}, f32[512,256]{1,0:T(8,128)S(1)}, u32[]{:S(2)}, u32[]{:S(2)}) collective-permute-start(f32[512,256]{1,0:T(8,128)S(1)} %copy.74), channel_id=1, source_target_pairs={{0,8},{8,0},{16,24},{24,16},{32,40},{40,32},{48,56},{56,48},{64,72... | collective-permute-start | bytes 1572872 | tf_op jit(solution)/shard_map/while/body/eval_jaxpr/cond/branch_0_fun/ppermute | solution.py:22
  153.5 1.3 copy-start.1
  153.5 1.5 copy-start.2
  153.6 1.7 %copy-start.4 = (f32[512,256]{0,1:T(8,128)S(1)}, f32[512,256]{0,1:T(8,128)}, u32[]{:S(2)}) copy-start(f32[512,256]{0,1:T(8,128)} %slice.299) | copy-start | bytes 1572868 | tf_op jit(solution)/shard_map/while
  158.2 3.1 %copy-start.3 = (f32[1536,256]{0,1:T(8,128)S(1)}, f32[1536,256]{0,1:T(8,128)}, u32[]{:S(2)}) copy-start(f32[1536,256]{0,1:T(8,128)} %get-tuple-element.365) | copy-start | bytes 4718596

commit v2 on v1

v2 whole, which is shorter than its diff:
```python
import jax
import jax.numpy as jnp
from jax import lax
from jax.experimental import pallas as pl
from jax.experimental.pallas import tpu as pltpu
from jax.sharding import PartitionSpec as P

COUPLE = 512
BOUND = 256
SENT = COUPLE + BOUND
ITERS = 4
ROWS = 256
LANES = 128
BITS = 5

ANY = pl.BlockSpec(memory_space=pltpu.HBM)
VMEM = pl.BlockSpec(memory_space=pltpu.VMEM)
SMEM = pl.BlockSpec(memory_space=pltpu.SMEM)


def f32(*shape):
    return jax.ShapeDtypeStruct(shape, jnp.float32)


def transfers(couple, ends, colour):
    areas = lax.axis_size("area")
    windows = lax.axis_size("win")
    onward = [(i, i + 1) for i in range(windows - 1)]

    def swap(bits):
        pairs = [(i, i ^ bits) for i in range(areas)]
        return lambda c, e: (lax.ppermute(c, "area", pairs), lax.ppermute(e, "win", onward))

    return lax.switch(colour - 1, [swap(bits) for bits in range(1, areas)], couple, ends)


def clip(total, low, high):
    width = total.shape[1] // LANES
    low, high = (jnp.concatenate([b] * width, axis=1) for b in (low, high))
    return jnp.minimum(jnp.maximum(total, low), high)


def prepare_kernel(area, partners, adjacency, lower, upper, halves, code, low, high, *unset):
    packed = 0
    for k in range(ITERS):
        mate = partners[k, area[0]]
        halves[k] = jnp.where(adjacency[area[0], mate] == 1, 0.5, 0.0)
        packed = packed + (partners[k, 0] << (BITS * k))
    code[0] = packed
    for source, target in ((lower, low), (upper, high)):
        for start in range(0, source.shape[1], LANES):
            line = source[0:1, start : start + LANES]
            target[start : start + LANES, :] = jnp.broadcast_to(line, (LANES, LANES)).T


def prepare(area, partners, adjacency, lower, upper, width):
    size = lower.shape[1]
    return pl.pallas_call(
        prepare_kernel,
        out_shape=(f32(ITERS), jax.ShapeDtypeStruct((1,), jnp.int32), f32(size, LANES), f32(size, LANES),
                   f32(size, width), f32(COUPLE, width), f32(BOUND, width)),
        in_specs=[SMEM, SMEM, SMEM, VMEM, VMEM],
        out_specs=(SMEM, SMEM, VMEM, VMEM, ANY, ANY, ANY),
        name="prepare",
    )(area, partners, adjacency, lower, upper)


def step_kernel(
    step_ref, halves, matrix_hbm, low_hbm, high_hbm, costs, total, other, before,
    total_out, couple, ends, matrix, low, high, v_ref, sems,
):
    size, width = total.shape
    blocks = size // ROWS
    at = lambda block: pl.ds(block * ROWS, ROWS)
    copies = lambda pairs, sem: [pltpu.make_async_copy(a, b, sem) for a, b in pairs]
    bounds = [copies([(low_hbm.at[at(i), :], low.at[at(i), :])], sems.at[0, i])
              + copies([(high_hbm.at[at(i), :], high.at[at(i), :])], sems.at[1, i]) for i in range(blocks)]
    rows_of = [copies([(matrix_hbm.at[at(i), :], matrix.at[at(i), :])], sems.at[2, i]) for i in range(blocks)]
    for group in bounds + rows_of:
        for copy in group:
            copy.start()
    now = step_ref[0]

    @pl.when(now == 0)
    def _():
        v_ref[...] = costs[...].astype(jnp.bfloat16)
        total_out[...] = jnp.zeros_like(total_out)
        for group in bounds:
            for copy in group:
                copy.wait()

    @pl.when(now > 0)
    def _():
        half = halves[jnp.maximum(now - 1, 0)]
        for i in range(blocks):
            for copy in bounds[i]:
                copy.wait()
            rows = slice(i * ROWS, (i + 1) * ROWS)
            t = total[rows, :]
            z = clip(t, low[rows, :], high[rows, :])
            if i < COUPLE // ROWS:
                z = z + half * (other[rows, :] - z)
            elif i == SENT // ROWS:
                z = 0.5 * (z + before[...])
            u = t - z
            v_ref[rows, :] = (costs[rows, :] + z - u).astype(jnp.bfloat16)
            total_out[rows, :] = u

    for i in range(blocks):
        for copy in rows_of[i]:
            copy.wait()
        rows = slice(i * ROWS, (i + 1) * ROWS)
        x = jnp.dot(matrix[rows, :], v_ref[...], preferred_element_type=jnp.float32)
        t = total_out[rows, :] + x
        total_out[rows, :] = t
        if i < COUPLE // ROWS:
            couple[rows, :] = clip(t, low[rows, :], high[rows, :])
        elif i < SENT // ROWS:
            ends[...] = clip(t, low[rows, :], high[rows, :])


def step(index, halves, matrix, low, high, costs, total, other, before):
    size, width = total.shape
    return pl.pallas_call(
        step_kernel,
        out_shape=(f32(size, width), f32(COUPLE, width), f32(BOUND, width)),
        in_specs=[SMEM, SMEM, ANY, ANY, ANY] + [VMEM] * 4,
        out_specs=(VMEM, VMEM, VMEM),
        input_output_aliases={6: 0},
        scratch_shapes=[
            pltpu.VMEM(matrix.shape, matrix.dtype),
            pltpu.VMEM(low.shape, jnp.float32),
            pltpu.VMEM(high.shape, jnp.float32),
            pltpu.VMEM((size, width), jnp.bfloat16),
            pltpu.SemaphoreType.DMA((3, size // ROWS)),
        ],
        compiler_params=pltpu.CompilerParams(vmem_limit_bytes=32 * 1024 * 1024),
        cost_estimate=pl.CostEstimate(
            flops=2 * size * size * width, bytes_accessed=2 * size * size + 20 * size * width, transcendentals=0
        ),
        name="step",
    )(index, halves, matrix, low, high, costs, total, other, before)


def finish_kernel(halves, low, high, total, other, before, z_out, u_out):
    half = halves[ITERS - 1]
    t = total[...]
    block = pl.program_id(0)
    y = clip(t, low[...], high[...])

    def put(z):
        z_out[...] = z
        u_out[...] = t - z

    @pl.when(block < COUPLE // ROWS)
    def _():
        put(y + half * (other[...] - y))

    @pl.when(block == SENT // ROWS)
    def _():
        put(0.5 * (y + before[...]))

    @pl.when((block >= COUPLE // ROWS) & (block != SENT // ROWS))
    def _():
        put(y)


def finish(halves, low, high, total, other, before):
    size, width = total.shape
    full = pl.BlockSpec((ROWS, width), lambda i: (i, 0))
    bound = pl.BlockSpec((ROWS, LANES), lambda i: (i, 0))
    return pl.pallas_call(
        finish_kernel,
        out_shape=(f32(size, width), f32(size, width)),
        grid=(size // ROWS,),
        in_specs=[
            SMEM,
            bound,
            bound,
            full,
            pl.BlockSpec((ROWS, width), lambda i: (jnp.minimum(i, COUPLE // ROWS - 1), 0)),
            pl.BlockSpec((ROWS, width), lambda i: (0, 0)),
        ],
        out_specs=(full, full),
        name="finish",
    )(halves, low, high, total, other, before)


def local(kkt, offsets, lower, upper, partners, adjacency):
    matrix = kkt[0, 0]
    costs = offsets[0, 0]
    area = lax.axis_index("area")[None].astype(jnp.int32)
    halves, code, low, high, total, other, before = prepare(
        area, partners, adjacency, lower[0], upper[0], costs.shape[1]
    )

    def iterate(k, carry):
        code, total, other, before = carry
        total, couple, ends = step(k[None], halves, matrix, low, high, costs, total, other, before)
        other, before = transfers(couple, ends, code & (2**BITS - 1))
        return code >> BITS, total, other, before

    _, total, other, before = lax.fori_loop(0, ITERS, iterate, (code[0], total, other, before))
    z_now, u_now = finish(halves, low, high, total, other, before)
    return (z_now[None, None], u_now[None, None])


def solution(mesh):
    in_specs = (
        P("area", "win", None, None),
        P("area", "win", None, None),
        P("area", "win", None),
        P("area", "win", None),
        P(),
        P(),
    )
    out_specs = (P("area", "win", None, None), P("area", "win", None, None))
    return jax.shard_map(local, mesh=mesh, in_specs=in_specs, out_specs=out_specs, check_vma=False)
```

time: 164 us -> 150 us (0.915); the launches traced: 163 us -> 152 us
  Pallas kernels: 0 us -> 38.8 us
  local copies, waits for them, and re-layouts: 33.1 us -> 0 us
  waiting for transfers between devices: 48.8 us -> 80.5 us
  other arithmetic: 28.8 us -> 0 us
  matrix products: 11.1 us -> 0 us
  starting transfers between devices: 30.5 us -> 25.8 us
  loops' own time: 10 us -> 6.54 us
    pallas_call x0 -> x6, Pallas kernels: none -> 38.8 us  [the longest x4 33 us: step(): pl.pallas_call(step_kernel, out_shape=(f32(size, width), f32(COUPLE, widt...]
    ppermute x8, waiting for transfers between devices: 48.8 us -> 80.5 us  [the longest x4 64.5 us: swap(): lax.ppermute(c, 'area', pairs)]
    sub x4 -> x0, other arithmetic: 12 us -> none  [iterate(): return (z_next, u_now + x_full - z_next)]
    convert_element_type x4 -> x0, other arithmetic: 11.7 us -> none  [iterate(): v_now = (costs + z_now - u_now).astype(jnp.bfloat16)]
    slice x20 -> x0, local copies, waits for them, and re-layouts: 11.5 us -> none  [the longest x4 7.47 us: iterate(): z_next = jnp.concatenate([new_couple, ends, starts, y_tail[BOUND:]], axis=0)]
    dot_general x8 -> x0, matrix products: 11.1 us -> none  [the longest x4 7.96 us: iterate(): x_head = jnp.dot(matrix[:sent], v_now, preferred_element_type=jnp.float32)]
    while x42 -> x0, local copies, waits for them, and re-layouts: 8.97 us -> none  [the longest x2 4.75 us: local(): lax.fori_loop(0, ITERS, iterate, (jnp.zeros_like(costs), jnp.zeros_like(c...]
    dynamic_slice x12 -> x0, local copies, waits for them, and re-layouts: 7.52 us -> none  [the longest x8 7.49 us: iterate(): linked = (adjacency[area, row[area]] == 1).astype(couple.dtype)]
  transfers between devices with their start and end apart: 8 -> 8, of which waited for: 4 -> 8; matrix products, arithmetic and copies ran while one was open for 10% -> 0% of each run, Pallas kernels for 0% -> 0%
where the time goes in v2:
time: 150 us; the launch traced here: 152 us
  waiting for transfers between devices  80.5 us (54%)
  Pallas kernels  38.8 us (26%)
  starting transfers between devices  25.8 us (17%)
  loops' own time  6.54 us (4%)
    ppermute x4, waiting for transfers between devices, swap(): lax.ppermute(c, 'area', pairs)  64.5 us
    pallas_call x4, Pallas kernels, step(): pl.pallas_call(step_kernel, out_shape=(f32(size, width), f32(COUPLE, widt...  33 us
    ppermute x4, waiting for transfers between devices, swap(): lax.ppermute(e, 'win', onward)  16.1 us
    ppermute x4, starting transfers between devices, swap(): lax.ppermute(e, 'win', onward)  14.4 us
    ppermute x4, starting transfers between devices, swap(): lax.ppermute(c, 'area', pairs)  11.4 us
    another operation x1, loops' own time, local(): lax.fori_loop(0, ITERS, iterate, (code[0], total, other, before))  6.33 us
    pallas_call x1, Pallas kernels, finish(): pl.pallas_call(finish_kernel, out_shape=(f32(size, width), f32(size, widt...  3.91 us
  transfers between devices with their start and end apart: 8, of which 8 were waited for; matrix products, arithmetic and copies ran while one was open for 0% of the time, Pallas kernels for 0%

profile of v2, /device:TPU:33, one launch (start us, length us, event | category | flops | bytes accessed | tf_op | source)
XLA Modules:
  0.0 152.2 jit_solution(4667701871204076378)
XLA Ops:
  0.6 1.8 %prepare.1 = (f32[4]{0:T(128)S(1)}, s32[1]{0:T(128)}, f32[1536,128]{1,0:T(8,128)S(1)}, f32[1536,128]{1,0:T(8,128)S(1)}, f32[1536,256]{1,0:T(8,128)S(1)}, /*index=5*/f32[512,256]{1,0:T(8,128)}, f32[256,256]{1,0:T(8,128)}) custom-call(s32[1]{0:T(128)} %bitcast.1.area, s32[4,32]{1,0:T(4,128)} %partners.1, s32[32,32]{1,0:T(8,128)} %adjacency.1, ...), custom_call_target="tpu_custom_call" | custom-call | tf_op jit(solution)/shard_map/prepare/pallas_call | solution.py:58
  2.5 145.8 %while.21 = (s32[]{:T(128)}, s32[]{:T(128)}, f32[1536,256]{1,0:T(8,128)S(1)}, f32[512,256]{1,0:T(8,128)}, f32[256,256]{1,0:T(8,128)}, /*index=5*/f32[4]{0:T(128)...) while((s32[]{:T(128)}, s32[]{:T(128)}, ...), condition=%wide.region_32.0_spmd, body=%wide.region_0.0_spmd.sunk | while | flops 1207959552 | bytes 15728961 | solution.py:203
  3.6 8.2 %step.8 = (f32[1536,256]{1,0:T(8,128)S(1)}, f32[512,256]{1,0:T(8,128)S(1)}, f32[256,256]{1,0:T(8,128)S(1)}) custom-call(s32[1]{0:T(128)} %bitcast.10.step_ref, f32[4]{0:T(128)S(1)} %get-tuple-element.644.halves, bf16[1536,1536]{1,0:T(8,128)(2,1)} %get-tuple-element.645.matrix_hbm, ...), custom_call_target="tpu_custom_call", output_to_operand_aliasing={{0}: (6, {})} | custom-call | flops 1207959552 | bytes 12582912 | tf_op jit(solution)/shard_map/while/body/eval_jaxpr/step/pallas_call | solution.py:124
  11.8 29.1 %conditional.2 = (f32[512,256]{1,0:T(8,128)}, f32[256,256]{1,0:T(8,128)}) conditional(s32[]{:T(128)} %clamp.11, (f32[512,256]{1,0:T(8,128)S(1)}, f32[256,256]{1,0:T(8,128)S(1)}) %tuple.165, (f32[512,256]{1,0:T(8,128)S(1)}, f32[256,256]{1,0:T(8,128)S(1)}) %tuple.165, (f32[512,256]{1,0:T(8,128)S(1)}, ...), branch_computations={%region_1.0_spmd, %region_2.0_spmd, %region_3.0_spmd, %region_4.0_... | conditional | bytes 3145824 | solution.py:34
  11.9 6.1 %collective-permute-start.30 = (f32[512,256]{1,0:T(8,128)S(1)}, f32[512,256]{1,0:T(8,128)}, u32[]{:S(2)}, u32[]{:S(2)}) collective-permute-start(f32[512,256]{1,0:T(8,128)S(1)} %get-tuple-element.380), channel_id=1, source_target_pairs={{0,128},{8,136},{16,144},{24,152},{32,160},{40,168},{48,176},{56,1... | collective-permute-start | bytes 1572872 | tf_op jit(solution)/shard_map/while/body/eval_jaxpr/cond/branch_15_fun/ppermute | solution.py:32
  18.0 3.8 %collective-permute-start.31 = (f32[256,256]{1,0:T(8,128)S(1)}, f32[256,256]{1,0:T(8,128)}, u32[]{:S(2)}, u32[]{:S(2)}) collective-permute-start(f32[256,256]{1,0:T(8,128)S(1)} %get-tuple-element.381), channel_id=1, source_target_pairs={{0,1},{1,2},{2,3},{3,4},{4,5},{5,6},{6,7},{8,9},{9,10},{10,11},{11... | collective-permute-start | bytes 786440 | tf_op jit(solution)/shard_map/while/body/eval_jaxpr/cond/branch_15_fun/ppermute | solution.py:32
  21.8 4.0 %collective-permute-done.31 = f32[256,256]{1,0:T(8,128)} collective-permute-done((f32[256,256]{1,0:T(8,128)S(1)}, f32[256,256]{1,0:T(8,128)}, u32[]{:S(2)}, u32[]{:S(2)}) %collective-permute-start.31) | collective-permute-done | bytes 262176 | tf_op jit(solution)/shard_map/while/body/eval_jaxpr/cond/branch_15_fun/ppermute | solution.py:32
  25.8 15.2 %collective-permute-done.30 = f32[512,256]{1,0:T(8,128)} collective-permute-done((f32[512,256]{1,0:T(8,128)S(1)}, f32[512,256]{1,0:T(8,128)}, u32[]{:S(2)}, u32[]{:S(2)}) %collective-permute-start.30) | collective-permute-done | bytes 524320 | tf_op jit(solution)/shard_map/while/body/eval_jaxpr/cond/branch_15_fun/ppermute | solution.py:32
  42.5 8.2 %step.8 = (f32[1536,256]{1,0:T(8,128)S(1)}, f32[512,256]{1,0:T(8,128)S(1)}, f32[256,256]{1,0:T(8,128)S(1)}) custom-call(s32[1]{0:T(128)} %bitcast.10.step_ref, f32[4]{0:T(128)S(1)} %get-tuple-element.644.halves, bf16[1536,1536]{1,0:T(8,128)(2,1)} %get-tuple-element.645.matrix_hbm, ...), custom_call_target="tpu_custom_call", output_to_operand_aliasing={{0}: (6, {})} | custom-call | flops 1207959552 | bytes 12582912 | tf_op jit(solution)/shard_map/while/body/eval_jaxpr/step/pallas_call | solution.py:124
  50.8 20.8 %conditional.2 = (f32[512,256]{1,0:T(8,128)}, f32[256,256]{1,0:T(8,128)}) conditional(s32[]{:T(128)} %clamp.11, (f32[512,256]{1,0:T(8,128)S(1)}, f32[256,256]{1,0:T(8,128)S(1)}) %tuple.165, (f32[512,256]{1,0:T(8,128)S(1)}, f32[256,256]{1,0:T(8,128)S(1)}) %tuple.165, (f32[512,256]{1,0:T(8,128)S(1)}, ...), branch_computations={%region_1.0_spmd, %region_2.0_spmd, %region_3.0_spmd, %region_4.0_... | conditional | bytes 3145824 | solution.py:34
  50.8 1.2 collective-permute-start.22
  52.0 3.8 %collective-permute-start.23 = (f32[256,256]{1,0:T(8,128)S(1)}, f32[256,256]{1,0:T(8,128)}, u32[]{:S(2)}, u32[]{:S(2)}) collective-permute-start(f32[256,256]{1,0:T(8,128)S(1)} %get-tuple-element.373), channel_id=1, source_target_pairs={{0,1},{1,2},{2,3},{3,4},{4,5},{5,6},{6,7},{8,9},{9,10},{10,11},{11... | collective-permute-start | bytes 786440 | tf_op jit(solution)/shard_map/while/body/eval_jaxpr/cond/branch_11_fun/ppermute | solution.py:32
  55.8 3.4 %collective-permute-done.23 = f32[256,256]{1,0:T(8,128)} collective-permute-done((f32[256,256]{1,0:T(8,128)S(1)}, f32[256,256]{1,0:T(8,128)}, u32[]{:S(2)}, u32[]{:S(2)}) %collective-permute-start.23) | collective-permute-done | bytes 262176 | tf_op jit(solution)/shard_map/while/body/eval_jaxpr/cond/branch_11_fun/ppermute | solution.py:32
  59.2 12.4 %collective-permute-done.22 = f32[512,256]{1,0:T(8,128)} collective-permute-done((f32[512,256]{1,0:T(8,128)S(1)}, f32[512,256]{1,0:T(8,128)}, u32[]{:S(2)}, u32[]{:S(2)}) %collective-permute-start.22) | collective-permute-done | bytes 524320 | tf_op jit(solution)/shard_map/while/body/eval_jaxpr/cond/branch_11_fun/ppermute | solution.py:32
  73.2 8.2 %step.8 = (f32[1536,256]{1,0:T(8,128)S(1)}, f32[512,256]{1,0:T(8,128)S(1)}, f32[256,256]{1,0:T(8,128)S(1)}) custom-call(s32[1]{0:T(128)} %bitcast.10.step_ref, f32[4]{0:T(128)S(1)} %get-tuple-element.644.halves, bf16[1536,1536]{1,0:T(8,128)(2,1)} %get-tuple-element.645.matrix_hbm, ...), custom_call_target="tpu_custom_call", output_to_operand_aliasing={{0}: (6, {})} | custom-call | flops 1207959552 | bytes 12582912 | tf_op jit(solution)/shard_map/while/body/eval_jaxpr/step/pallas_call | solution.py:124
  81.4 28.4 %conditional.2 = (f32[512,256]{1,0:T(8,128)}, f32[256,256]{1,0:T(8,128)}) conditional(s32[]{:T(128)} %clamp.11, (f32[512,256]{1,0:T(8,128)S(1)}, f32[256,256]{1,0:T(8,128)S(1)}) %tuple.165, (f32[512,256]{1,0:T(8,128)S(1)}, f32[256,256]{1,0:T(8,128)S(1)}) %tuple.165, (f32[512,256]{1,0:T(8,128)S(1)}, ...), branch_computations={%region_1.0_spmd, %region_2.0_spmd, %region_3.0_spmd, %region_4.0_... | conditional | bytes 3145824 | solution.py:34
  81.5 0.1 collective-permute-start.44
  81.6 3.8 %collective-permute-start.45 = (f32[256,256]{1,0:T(8,128)S(1)}, f32[256,256]{1,0:T(8,128)}, u32[]{:S(2)}, u32[]{:S(2)}) collective-permute-start(f32[256,256]{1,0:T(8,128)S(1)} %get-tuple-element.395), channel_id=1, source_target_pairs={{0,1},{1,2},{2,3},{3,4},{4,5},{5,6},{6,7},{8,9},{9,10},{10,11},{11... | collective-permute-start | bytes 786440 | tf_op jit(solution)/shard_map/while/body/eval_jaxpr/cond/branch_22_fun/ppermute | solution.py:32
  85.4 4.4 %collective-permute-done.45 = f32[256,256]{1,0:T(8,128)} collective-permute-done((f32[256,256]{1,0:T(8,128)S(1)}, f32[256,256]{1,0:T(8,128)}, u32[]{:S(2)}, u32[]{:S(2)}) %collective-permute-start.45) | collective-permute-done | bytes 262176 | tf_op jit(solution)/shard_map/while/body/eval_jaxpr/cond/branch_22_fun/ppermute | solution.py:32
  89.9 19.9 %collective-permute-done.44 = f32[512,256]{1,0:T(8,128)} collective-permute-done((f32[512,256]{1,0:T(8,128)S(1)}, f32[512,256]{1,0:T(8,128)}, u32[]{:S(2)}, u32[]{:S(2)}) %collective-permute-start.44) | collective-permute-done | bytes 524320 | tf_op jit(solution)/shard_map/while/body/eval_jaxpr/cond/branch_22_fun/ppermute | solution.py:32
  111.3 8.2 %step.8 = (f32[1536,256]{1,0:T(8,128)S(1)}, f32[512,256]{1,0:T(8,128)S(1)}, f32[256,256]{1,0:T(8,128)S(1)}) custom-call(s32[1]{0:T(128)} %bitcast.10.step_ref, f32[4]{0:T(128)S(1)} %get-tuple-element.644.halves, bf16[1536,1536]{1,0:T(8,128)(2,1)} %get-tuple-element.645.matrix_hbm, ...), custom_call_target="tpu_custom_call", output_to_operand_aliasing={{0}: (6, {})} | custom-call | flops 1207959552 | bytes 12582912 | tf_op jit(solution)/shard_map/while/body/eval_jaxpr/step/pallas_call | solution.py:124
  119.6 28.2 %conditional.2 = (f32[512,256]{1,0:T(8,128)}, f32[256,256]{1,0:T(8,128)}) conditional(s32[]{:T(128)} %clamp.11, (f32[512,256]{1,0:T(8,128)S(1)}, f32[256,256]{1,0:T(8,128)S(1)}) %tuple.165, (f32[512,256]{1,0:T(8,128)S(1)}, f32[256,256]{1,0:T(8,128)S(1)}) %tuple.165, (f32[512,256]{1,0:T(8,128)S(1)}, ...), branch_computations={%region_1.0_spmd, %region_2.0_spmd, %region_3.0_spmd, %region_4.0_... | conditional | bytes 3145824 | solution.py:34
  119.7 4.0 %collective-permute-start.26 = (f32[512,256]{1,0:T(8,128)S(1)}, f32[512,256]{1,0:T(8,128)}, u32[]{:S(2)}, u32[]{:S(2)}) collective-permute-start(f32[512,256]{1,0:T(8,128)S(1)} %get-tuple-element.376), channel_id=1, source_target_pairs={{0,112},{8,120},{16,96},{24,104},{32,80},{40,88},{48,64},{56,72},{... | collective-permute-start | bytes 1572872 | tf_op jit(solution)/shard_map/while/body/eval_jaxpr/cond/branch_13_fun/ppermute | solution.py:32
  123.6 2.9 %collective-permute-start.27 = (f32[256,256]{1,0:T(8,128)S(1)}, f32[256,256]{1,0:T(8,128)}, u32[]{:S(2)}, u32[]{:S(2)}) collective-permute-start(f32[256,256]{1,0:T(8,128)S(1)} %get-tuple-element.377), channel_id=1, source_target_pairs={{0,1},{1,2},{2,3},{3,4},{4,5},{5,6},{6,7},{8,9},{9,10},{10,11},{11... | collective-permute-start | bytes 786440 | tf_op jit(solution)/shard_map/while/body/eval_jaxpr/cond/branch_13_fun/ppermute | solution.py:32
  126.6 4.3 %collective-permute-done.27 = f32[256,256]{1,0:T(8,128)} collective-permute-done((f32[256,256]{1,0:T(8,128)S(1)}, f32[256,256]{1,0:T(8,128)}, u32[]{:S(2)}, u32[]{:S(2)}) %collective-permute-start.27) | collective-permute-done | bytes 262176 | tf_op jit(solution)/shard_map/while/body/eval_jaxpr/cond/branch_13_fun/ppermute | solution.py:32
  130.8 17.0 %collective-permute-done.26 = f32[512,256]{1,0:T(8,128)} collective-permute-done((f32[512,256]{1,0:T(8,128)S(1)}, f32[512,256]{1,0:T(8,128)}, u32[]{:S(2)}, u32[]{:S(2)}) %collective-permute-start.26) | collective-permute-done | bytes 524320 | tf_op jit(solution)/shard_map/while/body/eval_jaxpr/cond/branch_13_fun/ppermute | solution.py:32
  148.3 3.9 %finish.1 = (f32[1536,256]{1,0:T(8,128)}, f32[1536,256]{1,0:T(8,128)}) custom-call(f32[4]{0:T(128)S(1)} %get-tuple-element.657, f32[1536,128]{1,0:T(8,128)S(1)} %get-tuple-element.655, f32[1536,128]{1,0:T(8,128)S(1)} %get-tuple-element.656, f32[1536,256]{1,0:T(8,128)S(1)} %get-tuple-element.449.total, f32[512,256]{1,0:T(8,128)} %get-tuple-element.450.other, ...), custom_call_target="tpu_custom_call" | custom-call | tf_op jit(solution)/shard_map/finish/pallas_call | solution.py:172
Async XLA Ops:
  11.9 29.1 %collective-permute-start.30 = (f32[512,256]{1,0:T(8,128)S(1)}, f32[512,256]{1,0:T(8,128)}, u32[]{:S(2)}, u32[]{:S(2)}) collective-permute-start(f32[512,256]{1,0:T(8,128)S(1)} %get-tuple-element.380), channel_id=1, source_target_pairs={{0,128},{8,136},{16,144},{24,152},{32,160},{40,168},{48,176},{56,1... | collective-permute-start | bytes 1572872 | tf_op jit(solution)/shard_map/while/body/eval_jaxpr/cond/branch_15_fun/ppermute | solution.py:32
  18.0 7.8 %collective-permute-start.31 = (f32[256,256]{1,0:T(8,128)S(1)}, f32[256,256]{1,0:T(8,128)}, u32[]{:S(2)}, u32[]{:S(2)}) collective-permute-start(f32[256,256]{1,0:T(8,128)S(1)} %get-tuple-element.381), channel_id=1, source_target_pairs={{0,1},{1,2},{2,3},{3,4},{4,5},{5,6},{6,7},{8,9},{9,10},{10,11},{11... | collective-permute-start | bytes 786440 | tf_op jit(solution)/shard_map/while/body/eval_jaxpr/cond/branch_15_fun/ppermute | solution.py:32
  50.8 20.8 %collective-permute-start.22 = (f32[512,256]{1,0:T(8,128)S(1)}, f32[512,256]{1,0:T(8,128)}, u32[]{:S(2)}, u32[]{:S(2)}) collective-permute-start(f32[512,256]{1,0:T(8,128)S(1)} %get-tuple-element.372), channel_id=1, source_target_pairs={{0,96},{8,104},{16,112},{24,120},{32,64},{40,72},{48,80},{56,88},{... | collective-permute-start | bytes 1572872 | tf_op jit(solution)/shard_map/while/body/eval_jaxpr/cond/branch_11_fun/ppermute | solution.py:32
  52.0 7.2 %collective-permute-start.23 = (f32[256,256]{1,0:T(8,128)S(1)}, f32[256,256]{1,0:T(8,128)}, u32[]{:S(2)}, u32[]{:S(2)}) collective-permute-start(f32[256,256]{1,0:T(8,128)S(1)} %get-tuple-element.373), channel_id=1, source_target_pairs={{0,1},{1,2},{2,3},{3,4},{4,5},{5,6},{6,7},{8,9},{9,10},{10,11},{11... | collective-permute-start | bytes 786440 | tf_op jit(solution)/shard_map/while/body/eval_jaxpr/cond/branch_11_fun/ppermute | solution.py:32
  81.5 28.3 %collective-permute-start.44 = (f32[512,256]{1,0:T(8,128)S(1)}, f32[512,256]{1,0:T(8,128)}, u32[]{:S(2)}, u32[]{:S(2)}) collective-permute-start(f32[512,256]{1,0:T(8,128)S(1)} %get-tuple-element.394), channel_id=1, source_target_pairs={{0,184},{8,176},{16,168},{24,160},{32,152},{40,144},{48,136},{56,1... | collective-permute-start | bytes 1572872 | tf_op jit(solution)/shard_map/while/body/eval_jaxpr/cond/branch_22_fun/ppermute | solution.py:32
  81.6 8.3 %collective-permute-start.45 = (f32[256,256]{1,0:T(8,128)S(1)}, f32[256,256]{1,0:T(8,128)}, u32[]{:S(2)}, u32[]{:S(2)}) collective-permute-start(f32[256,256]{1,0:T(8,128)S(1)} %get-tuple-element.395), channel_id=1, source_target_pairs={{0,1},{1,2},{2,3},{3,4},{4,5},{5,6},{6,7},{8,9},{9,10},{10,11},{11... | collective-permute-start | bytes 786440 | tf_op jit(solution)/shard_map/while/body/eval_jaxpr/cond/branch_22_fun/ppermute | solution.py:32
  119.7 28.2 %collective-permute-start.26 = (f32[512,256]{1,0:T(8,128)S(1)}, f32[512,256]{1,0:T(8,128)}, u32[]{:S(2)}, u32[]{:S(2)}) collective-permute-start(f32[512,256]{1,0:T(8,128)S(1)} %get-tuple-element.376), channel_id=1, source_target_pairs={{0,112},{8,120},{16,96},{24,104},{32,80},{40,88},{48,64},{56,72},{... | collective-permute-start | bytes 1572872 | tf_op jit(solution)/shard_map/while/body/eval_jaxpr/cond/branch_13_fun/ppermute | solution.py:32
  123.6 7.2 %collective-permute-start.27 = (f32[256,256]{1,0:T(8,128)S(1)}, f32[256,256]{1,0:T(8,128)}, u32[]{:S(2)}, u32[]{:S(2)}) collective-permute-start(f32[256,256]{1,0:T(8,128)S(1)} %get-tuple-element.377), channel_id=1, source_target_pairs={{0,1},{1,2},{2,3},{3,4},{4,5},{5,6},{6,7},{8,9},{9,10},{10,11},{11... | collective-permute-start | bytes 786440 | tf_op jit(solution)/shard_map/while/body/eval_jaxpr/cond/branch_13_fun/ppermute | solution.py:32
